TPU v7x, 32 devices: a whole 2x2x4 slice. The times are simulated.
32 devices in a mesh: dp: 8 (over y, x, core), tensor: 4 (over z).
Axes of the slice: x: 2, y: 2, z: 4, core: 2. Of those that a mesh axis runs over, the one named last changes fastest.
Arguments:
- hidden_in: bfloat16 [16384, 1024], P('dp'), may hold values from -6 to 6
- lengths: int32 [8], P('dp'), may hold values from 512 to 2048, as said below
- query_weight: bfloat16 [1024, 1024], P(None, 'tensor'), may hold values from -0.1875 to 0.1875
- query_bias: bfloat16 [1024], P('tensor'), may hold values from -1 to 1
- key_weight: bfloat16 [1024, 1024], P(None, 'tensor'), may hold values from -0.1875 to 0.1875
- value_weight: bfloat16 [1024, 1024], P(None, 'tensor'), may hold values from -0.1875 to 0.1875
- value_bias: bfloat16 [1024], P('tensor'), may hold values from -1 to 1
- output_weight: bfloat16 [1024, 1024], P(None, 'tensor'), may hold values from -2 to 2
- output_bias: bfloat16 [1024], replicated, may hold values from -1 to 1
- first_gain: bfloat16 [1024], replicated, may hold values from 0.5 to 1.5
- first_shift: bfloat16 [1024], replicated, may hold values from -1 to 1
- inner_weight: bfloat16 [1024, 4096], P(None, 'tensor'), may hold values from -0.1875 to 0.1875
- inner_bias: bfloat16 [4096], P('tensor'), may hold values from -1 to 1
- outer_weight: bfloat16 [1024, 4096], P(None, 'tensor'), may hold values from -0.125 to 0.125
- outer_bias: bfloat16 [1024], replicated, may hold values from -1 to 1
- second_gain: bfloat16 [1024], replicated, may hold values from 0.5 to 1.5
- second_shift: bfloat16 [1024], replicated, may hold values from -1 to 1
- cotangent: bfloat16 [16384, 1024], P('dp'), may hold values from -6 to 6
- teacher: bfloat16 [16384, 1024], P('dp'), may hold values from -6 to 6
Outputs:
- layer_output: bfloat16 [16384, 1024], P(('dp', 'tensor'))
- distill_loss: float32 [], replicated
- input_grad: float32 [16384, 1024], P(('dp', 'tensor'))
- query_weight_grad: float32 [1024, 1024], P('dp', 'tensor')
- query_bias_grad: float32 [1024], replicated
- key_weight_grad: float32 [1024, 1024], P('dp', 'tensor')
- value_weight_grad: float32 [1024, 1024], P('dp', 'tensor')
- value_bias_grad: float32 [1024], replicated
- output_weight_grad: float32 [1024, 1024], P('dp', 'tensor')
- output_bias_grad: float32 [1024], replicated
- first_gain_grad: float32 [1024], replicated
- first_shift_grad: float32 [1024], replicated
- inner_weight_grad: float32 [1024, 4096], P('dp', 'tensor')
- inner_bias_grad: float32 [4096], replicated
- outer_weight_grad: float32 [1024, 4096], P('dp', 'tensor')
- outer_bias_grad: float32 [1024], replicated
- second_gain_grad: float32 [1024], replicated
- second_shift_grad: float32 [1024], replicated
Inputs may be any that keep to these rules, and one draw needn't show every extreme that they name: `lengths`: one sequence's valid tokens; slots after them are padding; some sequence fills all 2048 slots.
All inputs are finite; a program needn't handle non-finite values.
Results may differ from a plain program's by a relative error of at most 0.018.
Values may be sent and summed in bfloat16 or wider, within the bound.
No kernel may reach another device: no remote copies, remote signals or barrier semaphores. Data moves between devices by JAX's collectives and lax.ppermute only.
A program may use at most 256 MiB of HBM per device.

v0:
```python
import math
import jax
import jax.numpy as jnp
from jax import lax
from jax.sharding import PartitionSpec as P

HD = 64
epsilon = 1e-05


def matmul(former, latter):
    return jnp.dot(former, latter, preferred_element_type=jnp.float32)


def times_rows(former, latter):
    return lax.dot_general(
        former, latter, (((1,), (1,)), ((), ())), preferred_element_type=jnp.float32
    )


def over_rows(former, latter):
    return lax.dot_general(
        former, latter, (((0,), (0,)), ((), ())), preferred_element_type=jnp.float32
    )


def layer_norm(hidden, norm_gain, norm_shift):
    centered = hidden - jnp.mean(hidden, axis=-1, keepdims=True)
    inverse = lax.rsqrt(jnp.mean(centered * centered, axis=-1, keepdims=True) + epsilon)
    normal = centered * inverse
    return (normal * norm_gain + norm_shift, normal, inverse)


def norm_back(upstream, normal, inverse, norm_gain):
    scaled = upstream * norm_gain
    return inverse * (
        scaled
        - jnp.mean(scaled, axis=-1, keepdims=True)
        - normal * jnp.mean(scaled * normal, axis=-1, keepdims=True)
    )


def gelu_exact(values):
    return 0.5 * values * (1.0 + jax.scipy.special.erf(values * 0.7071067811865476))


def gelu_slope(values):
    return (
        0.5 * (1.0 + jax.scipy.special.erf(values * 0.7071067811865476))
        + values * jnp.exp(-0.5 * values * values) * 0.3989422804014327
    )


def split_blocks(queries, keys_all, values_all):
    seq_len, local_width = queries.shape
    heads_here = local_width // HD
    block_rows = min(512, seq_len)
    block_count = seq_len // block_rows
    keys_split = keys_all.reshape(seq_len, heads_here, HD)
    values_split = values_all.reshape(seq_len, heads_here, HD)
    query_blocks = queries.reshape(block_count, block_rows, heads_here, HD)
    return (keys_split, values_split, query_blocks, block_count, block_rows, heads_here)


def block_scores(query_block, keys_split, key_valid, score_scale):
    scores = (
        jnp.einsum("qhd,khd->hqk", query_block, keys_split, preferred_element_type=jnp.float32)
        * score_scale
    )
    return jnp.where(key_valid[None, None, :], scores, -1e30)


def attend_forward(queries, keys_all, values_all, key_valid, score_scale):
    keys_split, values_split, query_blocks, block_count, block_rows, heads_here = split_blocks(
        queries, keys_all, values_all
    )

    def one_block(query_block):
        scores = block_scores(query_block, keys_split, key_valid, score_scale)
        row_peak = jnp.max(scores, axis=-1, keepdims=True)
        exponent = jnp.exp(scores - row_peak)
        row_total = jnp.sum(exponent, axis=-1, keepdims=True)
        probs = (exponent / row_total).astype(jnp.bfloat16)
        context = jnp.einsum(
            "hqk,khd->qhd", probs, values_split, preferred_element_type=jnp.float32
        )
        return (context, (row_peak + jnp.log(row_total))[..., 0])

    context, logsum = lax.map(one_block, query_blocks)
    return (context.reshape(queries.shape), logsum)


def attend_backward(queries, keys_all, values_all, key_valid, score_scale, logsum, context_grad):
    keys_split, values_split, query_blocks, block_count, block_rows, heads_here = split_blocks(
        queries, keys_all, values_all
    )
    grad_blocks = context_grad.reshape(block_count, block_rows, heads_here, HD)

    def one_block(carry, inputs):
        key_sum, value_sum = carry
        query_block, grad_block, logsum_block = inputs
        scores = block_scores(query_block, keys_split, key_valid, score_scale)
        probs = jnp.exp(scores - logsum_block[..., None])
        prob_grad = jnp.einsum(
            "qhd,khd->hqk", grad_block, values_split, preferred_element_type=jnp.float32
        )
        centre = jnp.sum(probs * prob_grad, axis=-1, keepdims=True)
        score_grad = (probs * (prob_grad - centre)).astype(jnp.bfloat16)
        query_grad = (
            jnp.einsum("hqk,khd->qhd", score_grad, keys_split, preferred_element_type=jnp.float32)
            * score_scale
        )
        key_sum = (
            key_sum
            + jnp.einsum(
                "hqk,qhd->khd", score_grad, query_block, preferred_element_type=jnp.float32
            )
            * score_scale
        )
        value_sum = value_sum + jnp.einsum(
            "hqk,qhd->khd",
            probs.astype(jnp.bfloat16),
            grad_block,
            preferred_element_type=jnp.float32,
        )
        return ((key_sum, value_sum), query_grad)

    zero_block = jnp.zeros(keys_split.shape, jnp.float32)
    (key_sum, value_sum), query_grads = lax.scan(
        one_block, (zero_block, zero_block), (query_blocks, grad_blocks, logsum)
    )
    return (
        query_grads.reshape(queries.shape),
        key_sum.reshape(queries.shape),
        value_sum.reshape(queries.shape),
    )


def shards(
    hidden_in,
    lengths,
    query_weight,
    query_bias,
    key_weight,
    value_weight,
    value_bias,
    output_weight,
    output_bias,
    first_gain,
    first_shift,
    inner_weight,
    inner_bias,
    outer_weight,
    outer_bias,
    second_gain,
    second_shift,
    cotangent,
    teacher,
):
    seq_len, model_width = hidden_in.shape
    tensor_size = lax.axis_size("tensor")
    tensor_index = lax.axis_index("tensor")
    share_rows = seq_len // tensor_size
    row_start = tensor_index * share_rows
    score_scale = 1.0 / math.sqrt(HD)
    positions = jnp.arange(seq_len, dtype=jnp.int32)
    row_valid = positions < lengths[0]
    token_total = lax.psum(jnp.sum(lengths), "dp").astype(jnp.float32)
    grad_scale = seq_len * lax.axis_size("dp") / (2.0 * token_total)
    hidden_float = hidden_in.astype(jnp.float32)
    queries = (matmul(hidden_in, query_weight) + query_bias).astype(jnp.bfloat16)
    keys_all = matmul(hidden_in, key_weight).astype(jnp.bfloat16)
    values_all = (matmul(hidden_in, value_weight) + value_bias).astype(jnp.bfloat16)
    context, logsum = attend_forward(queries, keys_all, values_all, row_valid, score_scale)
    context_low = context.astype(jnp.bfloat16)
    attention_part = times_rows(context_low, output_weight)

    def take_own(array_in):
        return lax.dynamic_slice_in_dim(array_in, row_start, share_rows, 0)

    attention_whole = lax.psum(attention_part, "tensor")
    normed, normal_one, inverse_one = layer_norm(
        hidden_float + (attention_whole + output_bias), first_gain, first_shift
    )
    normed_low = normed.astype(jnp.bfloat16)
    inner = matmul(normed_low, inner_weight) + inner_bias
    activated = gelu_exact(inner).astype(jnp.bfloat16)
    outer_part = times_rows(activated, outer_weight)
    outer_rows = lax.psum(outer_part, "tensor")
    final, normal_two, inverse_two = layer_norm(
        normed + (outer_rows + outer_bias), second_gain, second_shift
    )
    row_mask = row_valid[:, None]
    difference = final - teacher.astype(jnp.float32)
    loss_part = jnp.sum(take_own(jnp.where(row_mask, difference * difference, 0.0)))
    final_grad = jnp.where(row_mask, cotangent.astype(jnp.float32) + grad_scale * difference, 0.0)
    second_grad = norm_back(final_grad, normal_two, inverse_two, second_gain)
    branch_low = second_grad.astype(jnp.bfloat16)
    activated_grad = matmul(branch_low, outer_weight)
    outer_weight_grad = over_rows(branch_low, activated)
    inner_low = (activated_grad * gelu_slope(inner)).astype(jnp.bfloat16)
    inner_bias_grad = jnp.sum(inner_low.astype(jnp.float32), axis=0)
    inner_weight_grad = over_rows(normed_low, inner_low)
    normed_part = times_rows(inner_low, inner_weight)
    normed_back = lax.psum(normed_part, "tensor")
    normed_grad = second_grad + normed_back
    first_grad = norm_back(normed_grad, normal_one, inverse_one, first_gain)
    attention_low = first_grad.astype(jnp.bfloat16)
    output_weight_grad = over_rows(attention_low, context_low)
    context_grad = matmul(attention_low, output_weight).astype(jnp.bfloat16)
    query_grad, key_grad, value_grad = attend_backward(
        queries, keys_all, values_all, row_valid, score_scale, logsum, context_grad
    )
    query_low = query_grad.astype(jnp.bfloat16)
    key_low = key_grad.astype(jnp.bfloat16)
    value_low = value_grad.astype(jnp.bfloat16)
    input_part = (
        times_rows(query_low, query_weight)
        + times_rows(key_low, key_weight)
        + times_rows(value_low, value_weight)
    )
    input_back = lax.psum(input_part.astype(jnp.bfloat16), "tensor").astype(jnp.float32)
    input_rows = take_own(input_back) + take_own(first_grad)
    weight_grads = (
        lax.psum_scatter(
            over_rows(hidden_in, query_low).astype(jnp.bfloat16),
            "dp",
            scatter_dimension=0,
            tiled=True,
        ).astype(jnp.float32),
        lax.psum_scatter(
            over_rows(hidden_in, key_low).astype(jnp.bfloat16),
            "dp",
            scatter_dimension=0,
            tiled=True,
        ).astype(jnp.float32),
        lax.psum_scatter(
            over_rows(hidden_in, value_low).astype(jnp.bfloat16),
            "dp",
            scatter_dimension=0,
            tiled=True,
        ).astype(jnp.float32),
        lax.psum_scatter(
            output_weight_grad.astype(jnp.bfloat16), "dp", scatter_dimension=0, tiled=True
        ).astype(jnp.float32),
        lax.psum_scatter(
            inner_weight_grad.astype(jnp.bfloat16), "dp", scatter_dimension=0, tiled=True
        ).astype(jnp.float32),
        lax.psum_scatter(
            outer_weight_grad.astype(jnp.bfloat16), "dp", scatter_dimension=0, tiled=True
        ).astype(jnp.float32),
    )

    def placed(vector_in):
        full_zeros = jnp.zeros((vector_in.shape[0] * tensor_size,), jnp.float32)
        return lax.dynamic_update_slice_in_dim(
            full_zeros, vector_in, tensor_index * vector_in.shape[0], 0
        )

    vector_grads = lax.psum(
        (
            placed(jnp.sum(query_low.astype(jnp.float32), axis=0)),
            placed(jnp.sum(value_low.astype(jnp.float32), axis=0)),
            jnp.sum(take_own(attention_low).astype(jnp.float32), axis=0),
            jnp.sum(take_own(normed_grad * normal_one), axis=0),
            jnp.sum(take_own(normed_grad), axis=0),
            placed(inner_bias_grad),
            jnp.sum(take_own(branch_low).astype(jnp.float32), axis=0),
            jnp.sum(take_own(final_grad * normal_two), axis=0),
            jnp.sum(take_own(final_grad), axis=0),
            loss_part,
        ),
        ("dp", "tensor"),
    )
    (
        query_bias_grad,
        value_bias_grad,
        output_bias_grad,
        first_gain_grad,
        first_shift_grad,
        inner_bias_full,
        outer_bias_grad,
        second_gain_grad,
        second_shift_grad,
        loss_total,
    ) = vector_grads
    (
        query_weight_grad,
        key_weight_grad,
        value_weight_grad,
        output_weight_sum,
        inner_weight_sum,
        outer_weight_sum,
    ) = weight_grads
    distill_loss = loss_total / token_total
    return (
        take_own(final).astype(jnp.bfloat16),
        distill_loss,
        input_rows,
        query_weight_grad,
        query_bias_grad,
        key_weight_grad,
        value_weight_grad,
        value_bias_grad,
        output_weight_sum,
        output_bias_grad,
        first_gain_grad,
        first_shift_grad,
        inner_weight_sum,
        inner_bias_full,
        outer_weight_sum,
        outer_bias_grad,
        second_gain_grad,
        second_shift_grad,
    )


def solution(mesh):
    in_specs = (
        P("dp", None),
        P("dp"),
        P(None, "tensor"),
        P("tensor"),
        P(None, "tensor"),
        P(None, "tensor"),
        P("tensor"),
        P(None, "tensor"),
        P(),
        P(),
        P(),
        P(None, "tensor"),
        P("tensor"),
        P(None, "tensor"),
        P(),
        P(),
        P(),
        P("dp", None),
        P("dp", None),
    )
    out_specs = (
        P(("dp", "tensor"), None),
        P(),
        P(("dp", "tensor"), None),
        P("dp", "tensor"),
        P(),
        P("dp", "tensor"),
        P("dp", "tensor"),
        P(),
        P("dp", "tensor"),
        P(),
        P(),
        P(),
        P("dp", "tensor"),
        P(),
        P("dp", "tensor"),
        P(),
        P(),
        P(),
    )
    return jax.shard_map(shards, mesh=mesh, in_specs=in_specs, out_specs=out_specs, check_vma=False)
```

profile of v0, /device:TPU:0, one launch (start us, length us, event | category | flops | bytes accessed | tf_op | source)
XLA Modules:
  0.0 1564.1 jit_solution(17279428161375169190)
XLA Ops:
  8.7 3.6 fusion.52
  14.1 4.0 copy.54
  18.1 3.7 convolution_convert_fusion.1
  25.2 55.2 %while.28 = (s32[]{:T(128)}, bf16[4,512,4,64]{1,3,2,0:T(8,128)(2,1)}, f32[4,4,512]{2,1,0:T(4,128)S(1)}, bf16[4,512,4,64]{1,3,2,0:T(8,128)(2,1)}, bf16[2048,4,64]...) while((s32[]{:T(128)}, bf16[4,512,4,64]{1,3,2,0:T(8,128)(2,1)}, ...), condition=%wide.region_3.4_spmd.clone, body=%wide.region_0.3_spmd.clone.sunk | while | flops 1124073472 | bytes 65872064 | solution.py:89
  25.9 3.5 fusion.136
  29.4 3.7 fusion.137
  33.2 4.9 fusion.138
  43.2 3.7 fusion.137
  47.0 4.9 fusion.138
  53.5 3.5 fusion.136
  57.0 3.7 fusion.137
  60.8 4.9 fusion.138
  70.8 3.7 fusion.137
  74.6 4.9 fusion.138
  83.8 5.6 fusion.70
  89.8 293.4 %all-reduce.6.cloned.1.call-done = f32[2048,1024]{1,0:T(8,128)} async-done(((f32[2048,1024]{1,0:T(8,128)}), f32[2048,1024]{1,0:T(8,128)}) %all-reduce.6.cloned.1.call-update) | async-done | bytes 8388624 | tf_op jit(solution)/shard_map/psum | solution.py:181
  383.2 5.9 fusion.54
  394.8 7.4 multiply_convert_fusion.1
  404.1 6.9 fusion.71
  411.0 8.8 psum.108
  421.3 279.7 %all-reduce.8.cloned.1.call-done = f32[2048,1024]{1,0:T(8,128)} async-done(((f32[2048,1024]{1,0:T(8,128)}), f32[2048,1024]{1,0:T(8,128)}) %all-reduce.8.cloned.1.call-update) | async-done | bytes 8388624 | tf_op jit(solution)/shard_map/psum | solution.py:189
  701.0 6.7 fusion.69
  708.8 10.9 multiply_reduce_fusion.6
  725.8 11.3 convert_reduce_fusion
  739.1 6.9 fusion.72
  746.5 9.4 convolution_convert_fusion.2
  756.0 10.5 convolution_convert_fusion.3
  766.7 269.2 %all-reduce.10.cloned.1.call-done = f32[2048,1024]{1,0:T(8,128)} async-done(((f32[2048,1024]{1,0:T(8,128)}), f32[2048,1024]{1,0:T(8,128)}) %all-reduce.10.cloned.1.call-update) | async-done | bytes 8388624 | tf_op jit(solution)/shard_map/psum | solution.py:205
  1036.0 16.3 %multiply_reduce_fusion.5 = (f32[2048]{0:T(1024)S(1)}, f32[2048]{0:T(1024)S(1)}, f32[2048,1024]{1,0:T(8,128)}) fusion(f32[1024]{0:T(1024)S(1)} %convert_element_type.183, f32[2048,1024]{1,0:T(8,128)} %copy-done.5, f32[2048,1024]{1,0:T(8,128)} %all-reduce.10.cloned.1.call-done, f32[2048,1024]{1,0:T(8,128)} %copy-done.7, f32[2048]{0:T(1024)S(1)} %get-tuple-element.345, ...), kind=kLoop, calls=%fused_computation.76 | loop fusion | flops 20967424 | bytes 41992192 | tf_op jit(solution)/shard_map/reduce_sum | solution.py:38
  1052.4 9.8 fusion.67
  1066.3 4.4 reshape.147
  1070.8 4.1 copy.58
  1076.0 166.5 %while.29 = (s32[]{:T(128)}, f32[2048,4,64]{0,2,1:T(8,128)S(1)}, f32[2048,4,64]{0,2,1:T(8,128)}, bf16[4,512,4,64]{1,3,2,0:T(8,128)(2,1)}, bf16[4,512,4,64]{1,3,2...) while((s32[]{:T(128)}, f32[2048,4,64]{0,2,1:T(8,128)S(1)}, ...), condition=%wide.region_20.21_spmd.clone, body=%wide.region_18.20_spmd.clone.sunk | while | flops 2750021632 | bytes 180945136 | solution.py:129
  1077.2 3.7 fusion.148
  1080.9 5.8 fusion.150
  1086.7 10.1 multiply_reduce_fusion.8
  1096.8 11.0 multiply_convert_fusion.3
  1107.8 7.2 fusion.151
  1118.9 3.7 fusion.148
  1122.6 6.2 fusion.150
  1128.8 9.9 multiply_reduce_fusion.8
  1138.7 10.6 multiply_convert_fusion.3
  1149.3 7.1 fusion.151
  1160.3 3.7 fusion.148
  1164.0 6.2 fusion.150
  1170.2 9.9 multiply_reduce_fusion.8
  1180.1 10.6 multiply_convert_fusion.3
  1190.7 7.1 fusion.151
  1201.8 3.7 fusion.148
  1205.5 6.2 fusion.150
  1211.7 9.9 multiply_reduce_fusion.8
  1221.6 10.6 multiply_convert_fusion.3
  1232.2 7.1 fusion.151
  1257.7 3.5 fusion.61
  1262.3 5.7 fusion.74
  1268.0 4.4 convolution_convert_fusion.4
  1272.5 4.5 fusion.73
  1277.1 9.1 add_convert_fusion
  1291.3 4.6 dynamic-slice_reduce_fusion
  1304.3 40.3 %all-reduce = (f32[]{:T(128)}, f32[1024]{0:T(1024)}, f32[1024]{0:T(1024)}, f32[1024]{0:T(1024)}, f32[1024]{0:T(1024)}, /*index=5*/f32[1024]{0:T(1024)}, f32[4096...) all-reduce(f32[]{:T(128)} %get-tuple-element.344, ...), channel_id=1, replica_groups=mesh['dp'=8,'tensor'=4] {'dp','tensor'}, use_global_device_ids=true, to_apply=%region_11.12 | all-reduce | flops 12289 | bytes 98312 | tf_op jit(solution)/shard_map/psum | solution.py:260
  1348.7 8.8 reduce-scatter.23.cloned.1.call-done
  1359.3 35.5 %reduce-scatter.13.cloned.1.call-done = bf16[128,256]{1,0:T(8,128)(2,1)} async-done(((bf16[1024,256]{1,0:T(8,128)(2,1)}), bf16[128,256]{1,0:T(8,128)(2,1)}) %reduce-scatter.13.cloned.1.call-update) | async-done | bytes 65552 | tf_op jit(solution)/shard_map/reduce_scatter | solution.py:243
  1396.3 155.7 %all-reduce.12.cloned.1.call-done = bf16[2048,1024]{1,0:T(8,128)(2,1)} async-done(((bf16[2048,1024]{1,0:T(8,128)(2,1)}), bf16[2048,1024]{1,0:T(8,128)(2,1)}) %all-reduce.12.cloned.1.call-update) | async-done | bytes 4194320 | tf_op jit(solution)/shard_map/psum | solution.py:222
  1552.0 3.6 dynamic-slice_add_fusion
  (225 shorter events, 98.7 us)
Async XLA Ops:
  7.2 387.5 %copy-start = (bf16[1024,1024]{1,0:T(8,128)(2,1)S(1)}, bf16[1024,1024]{1,0:T(8,128)(2,1)}, u32[]{:S(2)}) copy-start(bf16[1024,1024]{1,0:T(8,128)(2,1)} %param.34) | copy-start | bytes 6291460
  7.2 376.0 %all-reduce.6.cloned.1.call-start = ((), (), s32[]{:S(2)}) async-start(), calls=%async_computation.6 | async-start | bytes 16777216 | tf_op jit(solution)/shard_map/psum | solution.py:181
  18.1 3.8 copy-start.9
  18.1 3.8 copy-start.25
  29.4 3.8 copy-start.11
  29.4 3.8 copy-start.21
  43.2 3.8 copy-start.11
  43.2 3.8 copy-start.21
  57.0 3.8 copy-start.11
  57.0 3.8 copy-start.21
  65.7 1.0 copy-start.22
  70.8 3.8 copy-start.11
  70.8 3.8 copy-start.21
  82.8 1.1 copy-start.15
  83.8 5.9 copy-start.29
  83.8 5.9 copy-start.30
  83.8 6.0 copy-start.31
  83.8 6.0 copy-start.32
  89.5 611.5 %all-reduce.8.cloned.1.call-start = ((), (), s32[]{:S(2)}) async-start(), calls=%async_computation.7 | async-start | bytes 16777216 | tf_op jit(solution)/shard_map/psum | solution.py:189
  383.2 7.0 copy-start.8
  383.2 8.2 copy-start.10
  394.7 7.4 copy-start.5
  394.8 9.3 copy-start.36
  402.1 1.9 copy-start.38
  411.0 10.2 copy-start.33
  411.0 10.2 copy-start.34
  411.0 10.2 copy-start.35
  411.0 625.0 %all-reduce.10.cloned.1.call-start = ((), (), s32[]{:S(2)}) async-start(), calls=%async_computation.8 | async-start | bytes 16777216 | tf_op jit(solution)/shard_map/psum | solution.py:205
  421.3 287.5 %copy-start.27 = (pred[2048]{0:T(1024)(128)(4,1)}, pred[2048]{0:T(1024)(128)(4,1)S(1)}, u32[]{:S(2)}) copy-start(pred[2048]{0:T(1024)(128)(4,1)S(1)} %iota_compare_fusion.2) | copy-start | bytes 6148
  719.7 3.5 copy-start.6
  719.7 6.1 copy-start.7
  719.7 6.1 copy-start.37
  725.8 11.3 copy-start.13
  737.1 2.0 copy-start.39
  746.0 549.9 %reduce-scatter.17.cloned.1.call-start = ((), (), s32[]{:S(2)}) async-start(), calls=%async_computation.12 | async-start | bytes 2359296 | tf_op jit(solution)/shard_map/reduce_scatter | solution.py:249
  756.0 541.7 %reduce-scatter.15.cloned.1.call-start = ((), (), s32[]{:S(2)}) async-start(), calls=%async_computation.11 | async-start | bytes 2359296 | tf_op jit(solution)/shard_map/reduce_scatter | solution.py:246
  766.5 578.7 %reduce-scatter.19.cloned.1.call-start = ((), (), s32[]{:S(2)}) async-start(), calls=%async_computation.13 | async-start | bytes 589824
  1052.3 11.8 copy-start.23
  1062.1 2.0 copy-start.14
  1076.2 1.0 copy-start.3
  1107.8 7.2 copy-start.2
  1115.0 2.9 copy-start.4
  1117.9 1.0 copy-start.3
  1149.3 7.1 copy-start.2
  1156.5 2.9 copy-start.4
  1159.3 1.0 copy-start.3
  1190.7 7.2 copy-start.2
  1197.9 2.9 copy-start.4
  1200.8 1.0 copy-start.3
  1232.2 7.2 copy-start.2
  1239.3 2.9 copy-start.4
  1244.8 1.0 copy-start.17
  1250.3 96.8 %reduce-scatter.21.cloned.1.call-start = ((), (), s32[]{:S(2)}) async-start(), calls=%async_computation.14 | async-start | bytes 589824
  1256.8 100.8 %reduce-scatter.23.cloned.1.call-start = ((), (), s32[]{:S(2)}) async-start(), calls=%async_computation.15 | async-start | bytes 589824
  1261.2 6.8 copy-start.16
  1262.3 10.2 copy-start.18
  1267.9 4.5 copy-start.24
  1267.9 126.8 %reduce-scatter.13.cloned.1.call-start = ((), (), s32[]{:S(2)}) async-start(), calls=%async_computation.10 | async-start | bytes 589824 | tf_op jit(solution)/shard_map/reduce_scatter | solution.py:243
  1272.5 4.6 copy-start.20
  1272.5 4.6 copy-start.26
  1277.0 10.1 copy-start.28
  1277.0 275.0 %all-reduce.12.cloned.1.call-start = ((), (), s32[]{:S(2)}) async-start(), calls=%async_computation.9 | async-start | bytes 8388608 | tf_op jit(solution)/shard_map/psum | solution.py:222
  1286.2 13.3 copy-start.12
  1291.3 264.3 %copy-start.1 = (bf16[1024,1024]{1,0:T(8,128)(2,1)S(1)}, bf16[1024,1024]{1,0:T(8,128)(2,1)}, u32[]{:S(2)}) copy-start(bf16[1024,1024]{1,0:T(8,128)(2,1)} %param.34) | copy-start | bytes 6291460
  (4 other events, 3.9 us)
Sparse Core Ops, SparseCore 0:
  89.6 293.5 all-reduce.5
  411.1 289.7 all-reduce.7
  746.1 289.8 all-reduce.9
  1039.1 40.0 reduce-scatter.16
  1082.4 41.1 reduce-scatter.14
  1250.4 32.5 reduce-scatter.18
  1286.1 34.2 reduce-scatter.20
  1323.4 34.0 reduce-scatter.22
  1360.6 34.0 reduce-scatter.12
  1397.0 154.9 all-reduce.11
where the time goes:
time: 1570 us; the launch traced here: 1560 us
  waiting for transfers between devices  1040 us (66%)
  matrix products  256 us (16%)
  other arithmetic  142 us (9%)
  local copies, waits for them, and re-layouts  53.8 us (3%)
  blocking collectives  49.1 us (3%)
  between operations  18.3 us (1%)
    psum x1, waiting for transfers between devices, shards(): attention_whole = lax.psum(attention_part, 'tensor')  293 us
    psum x1, waiting for transfers between devices, shards(): outer_rows = lax.psum(outer_part, 'tensor')  280 us
    psum x1, waiting for transfers between devices, shards(): normed_back = lax.psum(normed_part, 'tensor')  269 us
    psum x1, waiting for transfers between devices, shards(): lax.psum(input_part.astype(jnp.bfloat16), 'tensor').astype(jnp.float32)  156 us
    convert_element_type x4, other arithmetic, one_block(): score_grad = (probs * (prob_grad - centre)).astype(jnp.bfloat16)  42.8 us
    psum x1, blocking collectives, shards(): lax.psum((placed(jnp.sum(query_low.astype(jnp.float32), axis=0)), placed(...  40.3 us
    dot_general x4, matrix products, one_block(): jnp.einsum('qhd,khd->hqk', grad_block, values_split, preferred_element_ty...  39.8 us
    dot_general x6, matrix products, times_rows(): lax.dot_general(former, latter, (((1,), (1,)), ((), ())), preferred_eleme...  38.7 us
  transfers between devices with their start and end apart: 10, of which 6 were waited for; matrix products, arithmetic and copies ran while one was open for 18% of the time, Pallas kernels for 0%

commit v1 on v0

--- a/solution.py
+++ b/solution.py
@@ -6,6 +6,10 @@
 
 HD = 64
 epsilon = 1e-05
+
+
+def perform_loads(mine):
+    return lax.all_gather(mine, "tensor").sum(axis=0)
 
 
 def matmul(former, latter):
@@ -178,7 +182,7 @@
     def take_own(array_in):
         return lax.dynamic_slice_in_dim(array_in, row_start, share_rows, 0)
 
-    attention_whole = lax.psum(attention_part, "tensor")
+    attention_whole = perform_loads(attention_part)
     normed, normal_one, inverse_one = layer_norm(
         hidden_float + (attention_whole + output_bias), first_gain, first_shift
     )

time: 1570 us -> 1860 us (1.18)
  waiting for transfers between devices: 1040 us -> 1310 us
    all_gather x0 -> x1, waiting for transfers between devices: none -> 564 us  [perform_loads(): return lax.all_gather(mine, 'tensor').sum(axis=0)]
    psum x1 -> x0, waiting for transfers between devices: 293 us -> none  [shards(): attention_whole = lax.psum(attention_part, 'tensor')]
  transfers between devices with their start and end apart: 10 -> 10, of which waited for: 6 -> 6; matrix products, arithmetic and copies ran while one was open for 18% -> 15% of each run, Pallas kernels for 0% -> 0%
where the time goes in v1:
time: 1860 us; the launch traced here: 1850 us
  waiting for transfers between devices  1310 us (70%)
  matrix products  257 us (14%)
  other arithmetic  157 us (8%)
  local copies, waits for them, and re-layouts  50.9 us (3%)
  blocking collectives  49.6 us (3%)
    all_gather x1, waiting for transfers between devices, perform_loads(): return lax.all_gather(mine, 'tensor').sum(axis=0)  564 us
    psum x1, waiting for transfers between devices, shards(): outer_rows = lax.psum(outer_part, 'tensor')  279 us
    psum x1, waiting for transfers between devices, shards(): normed_back = lax.psum(normed_part, 'tensor')  270 us
    psum x1, waiting for transfers between devices, shards(): lax.psum(input_part.astype(jnp.bfloat16), 'tensor').astype(jnp.float32)  156 us
    convert_element_type x4, other arithmetic, one_block(): score_grad = (probs * (prob_grad - centre)).astype(jnp.bfloat16)  42.8 us
    psum x1, blocking collectives, shards(): lax.psum((placed(jnp.sum(query_low.astype(jnp.float32), axis=0)), placed(...  40.5 us
    dot_general x6, matrix products, times_rows(): lax.dot_general(former, latter, (((1,), (1,)), ((), ())), preferred_eleme...  38.7 us
    dot_general x4, matrix products, one_block(): jnp.einsum('qhd,khd->hqk', grad_block, values_split, preferred_element_ty...  37.5 us
  transfers between devices with their start and end apart: 10, of which 6 were waited for; matrix products, arithmetic and copies ran while one was open for 15% of the time, Pallas kernels for 0%

profile of v1, /device:TPU:0, one launch (start us, length us, event | category | flops | bytes accessed | tf_op | source)
XLA Modules:
  0.0 1847.1 jit_solution(13994985651124538956)
XLA Ops:
  8.7 3.6 fusion.52
  14.1 4.0 copy.54
  18.1 3.7 convolution_convert_fusion.1
  25.3 55.2 %while.28 = (s32[]{:T(128)}, bf16[4,512,4,64]{1,3,2,0:T(8,128)(2,1)}, f32[4,4,512]{2,1,0:T(4,128)}, bf16[4,512,4,64]{1,3,2,0:T(8,128)(2,1)}, bf16[2048,4,64]{0,2...) while((s32[]{:T(128)}, bf16[4,512,4,64]{1,3,2,0:T(8,128)(2,1)}, ...), condition=%wide.region_3.4_spmd.clone, body=%wide.region_0.3_spmd.clone.sunk | while | flops 1124073472 | bytes 65872064 | solution.py:93
  25.9 3.5 fusion.136
  29.5 3.7 fusion.137
  33.2 4.9 fusion.138
  43.3 3.7 fusion.137
  47.0 4.9 fusion.138
  53.6 3.5 fusion.136
  57.1 3.7 fusion.137
  60.8 4.9 fusion.138
  70.9 3.7 fusion.137
  74.7 4.9 fusion.138
  84.2 5.6 fusion.70
  90.3 563.8 %all-gather.3.cloned.1.call-done = f32[8192,1024]{1,0:T(8,128)} async-done(((f32[2048,1024]{1,0:T(8,128)}), f32[8192,1024]{1,0:T(8,128)}) %all-gather.3.cloned.1.call-update) | async-done | bytes 33554448 | tf_op jit(solution)/shard_map/all_gather | solution.py:12
  654.1 16.4 reduce_sum.197
  670.5 5.9 fusion.54
  682.1 7.4 multiply_convert_fusion.1
  691.4 6.9 fusion.71
  698.4 9.1 psum.100
  708.9 278.6 %all-reduce.5.cloned.1.call-done = f32[2048,1024]{1,0:T(8,128)} async-done(((f32[2048,1024]{1,0:T(8,128)}), f32[2048,1024]{1,0:T(8,128)}) %all-reduce.5.cloned.1.call-update) | async-done | bytes 8388624 | tf_op jit(solution)/shard_map/psum | solution.py:193
  987.5 6.7 fusion.69
  995.4 10.9 multiply_reduce_fusion.6
  1012.3 11.4 convert_reduce_fusion
  1025.7 6.9 fusion.72
  1032.8 9.4 convolution_convert_fusion.2
  1042.3 10.5 convolution_convert_fusion.3
  1052.9 269.7 %all-reduce.7.cloned.1.call-done = f32[2048,1024]{1,0:T(8,128)} async-done(((f32[2048,1024]{1,0:T(8,128)}), f32[2048,1024]{1,0:T(8,128)}) %all-reduce.7.cloned.1.call-update) | async-done | bytes 8388624 | tf_op jit(solution)/shard_map/psum | solution.py:209
  1322.6 13.0 multiply_reduce_fusion.5
  1335.7 9.5 fusion.67
  1350.4 4.0 copy.58
  1355.7 169.6 %while.29 = (s32[]{:T(128)}, f32[2048,4,64]{0,2,1:T(8,128)}, f32[2048,4,64]{0,2,1:T(8,128)}, bf16[4,512,4,64]{1,3,2,0:T(8,128)(2,1)}, bf16[4,512,4,64]{1,3,2,0:T...) while((s32[]{:T(128)}, f32[2048,4,64]{0,2,1:T(8,128)}, ...), condition=%wide.region_20.21_spmd.clone, body=%wide.region_18.20_spmd.clone.sunk | while | flops 2750021632 | bytes 172556464 | solution.py:133
  1360.5 5.8 fusion.150
  1366.3 9.4 multiply_reduce_fusion.8
  1375.8 11.0 multiply_convert_fusion.3
  1386.7 7.1 fusion.151
  1393.8 3.9 fusion.149
  1402.4 6.2 fusion.150
  1408.6 9.4 multiply_reduce_fusion.8
  1417.9 10.6 multiply_convert_fusion.3
  1428.6 6.9 fusion.151
  1435.5 4.6 fusion.149
  1444.8 6.2 fusion.150
  1451.0 9.4 multiply_reduce_fusion.8
  1460.3 10.6 multiply_convert_fusion.3
  1470.9 6.9 fusion.151
  1477.8 4.6 fusion.149
  1487.2 6.2 fusion.150
  1493.4 9.4 multiply_reduce_fusion.8
  1502.7 10.6 multiply_convert_fusion.3
  1513.3 6.9 fusion.151
  1520.2 4.6 fusion.149
  1540.7 3.5 fusion.61
  1545.2 5.7 fusion.74
  1551.0 4.5 convolution_convert_fusion.4
  1555.5 4.5 fusion.73
  1560.1 9.1 add_convert_fusion
  1574.2 4.6 dynamic-slice_reduce_fusion
  1587.2 40.5 %all-reduce = (f32[]{:T(128)}, f32[1024]{0:T(1024)}, f32[1024]{0:T(1024)}, f32[1024]{0:T(1024)}, f32[1024]{0:T(1024)}, /*index=5*/f32[1024]{0:T(1024)}, f32[4096...) all-reduce(f32[]{:T(128)} %get-tuple-element.344, ...), channel_id=1, replica_groups=mesh['dp'=8,'tensor'=4] {'dp','tensor'}, use_global_device_ids=true, to_apply=%region_11.12 | all-reduce | flops 12289 | bytes 98312 | tf_op jit(solution)/shard_map/psum | solution.py:264
  1631.8 9.0 reduce-scatter.23.cloned.1.call-done
  1642.5 35.5 %reduce-scatter.13.cloned.1.call-done = bf16[128,256]{1,0:T(8,128)(2,1)} async-done(((bf16[1024,256]{1,0:T(8,128)(2,1)}), bf16[128,256]{1,0:T(8,128)(2,1)}) %reduce-scatter.13.cloned.1.call-update) | async-done | bytes 65552 | tf_op jit(solution)/shard_map/reduce_scatter | solution.py:247
  1679.6 155.7 %all-reduce.9.cloned.1.call-done = bf16[2048,1024]{1,0:T(8,128)(2,1)} async-done(((bf16[2048,1024]{1,0:T(8,128)(2,1)}), bf16[2048,1024]{1,0:T(8,128)(2,1)}) %all-reduce.9.cloned.1.call-update) | async-done | bytes 4194320 | tf_op jit(solution)/shard_map/psum | solution.py:226
  1835.3 3.6 dynamic-slice_add_fusion
  (220 shorter events, 103.1 us)
Async XLA Ops:
  7.2 674.9 %copy-start = (bf16[1024,1024]{1,0:T(8,128)(2,1)S(1)}, bf16[1024,1024]{1,0:T(8,128)(2,1)}, u32[]{:S(2)}) copy-start(bf16[1024,1024]{1,0:T(8,128)(2,1)} %param.34) | copy-start | bytes 6291460
  7.2 646.9 %all-gather.3.cloned.1.call-start = ((), (), s32[]{:S(2)}) async-start(), calls=%async_computation.12 | async-start | bytes 41943040 | tf_op jit(solution)/shard_map/all_gather | solution.py:12
  18.1 3.8 copy-start.11
  18.1 3.8 copy-start.28
  29.4 3.8 copy-start.13
  29.4 3.8 copy-start.24
  38.1 1.0 copy-start.25
  43.2 3.8 copy-start.13
  43.3 3.8 copy-start.24
  51.9 1.0 copy-start.25
  57.1 3.8 copy-start.13
  57.1 3.8 copy-start.24
  65.7 1.0 copy-start.25
  70.9 3.8 copy-start.13
  70.9 3.8 copy-start.24
  79.6 1.0 copy-start.25
  80.5 9.3 copy-start.3
  83.2 1.0 copy-start.18
  84.2 6.0 copy-start.32
  84.2 6.0 copy-start.33
  84.2 6.0 copy-start.34
  84.2 6.0 copy-start.35
  89.9 897.6 %all-reduce.5.cloned.1.call-start = ((), (), s32[]{:S(2)}) async-start(), calls=%async_computation.6 | async-start | bytes 16777216 | tf_op jit(solution)/shard_map/psum | solution.py:193
  670.5 7.0 copy-start.6
  670.5 8.2 copy-start.12
  682.1 7.4 copy-start.5
  682.1 9.3 copy-start.39
  689.5 1.9 copy-start.41
  698.3 10.5 copy-start.36
  698.3 10.5 copy-start.37
  698.3 10.5 copy-start.38
  698.3 624.2 %all-reduce.7.cloned.1.call-start = ((), (), s32[]{:S(2)}) async-start(), calls=%async_computation.7 | async-start | bytes 16777216 | tf_op jit(solution)/shard_map/psum | solution.py:209
  708.9 286.5 %copy-start.30 = (pred[2048]{0:T(1024)(128)(4,1)}, pred[2048]{0:T(1024)(128)(4,1)S(1)}, u32[]{:S(2)}) copy-start(pred[2048]{0:T(1024)(128)(4,1)S(1)} %iota_compare_fusion.2) | copy-start | bytes 6148
  1006.3 3.5 copy-start.7
  1006.3 6.1 copy-start.8
  1006.3 6.1 copy-start.40
  1012.3 11.4 copy-start.16
  1023.7 2.0 copy-start.42
  1032.6 546.2 %reduce-scatter.17.cloned.1.call-start = ((), (), s32[]{:S(2)}) async-start(), calls=%async_computation.11 | async-start | bytes 2359296 | tf_op jit(solution)/shard_map/reduce_scatter | solution.py:253
  1042.2 538.3 %reduce-scatter.15.cloned.1.call-start = ((), (), s32[]{:S(2)}) async-start(), calls=%async_computation.10 | async-start | bytes 2359296 | tf_op jit(solution)/shard_map/reduce_scatter | solution.py:250
  1052.8 575.5 %reduce-scatter.19.cloned.1.call-start = ((), (), s32[]{:S(2)}) async-start(), calls=%async_computation.13 | async-start | bytes 589824
  1335.6 9.6 copy-start.10
  1335.6 11.7 copy-start.26
  1345.2 2.1 copy-start.17
  1345.2 10.5 copy-start.4
  1345.2 10.5 copy-start.14
  1386.7 7.1 copy-start.2
  1428.6 6.9 copy-start.2
  1470.9 6.9 copy-start.2
  1513.3 6.9 copy-start.2
  1525.3 8.0 copy-start.9
  1527.7 1.0 copy-start.20
  1533.2 96.9 %reduce-scatter.21.cloned.1.call-start = ((), (), s32[]{:S(2)}) async-start(), calls=%async_computation.14 | async-start | bytes 589824
  1539.7 101.1 %reduce-scatter.23.cloned.1.call-start = ((), (), s32[]{:S(2)}) async-start(), calls=%async_computation.15 | async-start | bytes 589824
  1544.2 6.8 copy-start.19
  1545.2 10.3 copy-start.21
  1550.9 4.6 copy-start.27
  1550.9 127.1 %reduce-scatter.13.cloned.1.call-start = ((), (), s32[]{:S(2)}) async-start(), calls=%async_computation.9 | async-start | bytes 589824 | tf_op jit(solution)/shard_map/reduce_scatter | solution.py:247
  1555.5 4.6 copy-start.23
  1555.5 4.6 copy-start.29
  1560.0 10.1 copy-start.31
  1560.1 275.3 %all-reduce.9.cloned.1.call-start = ((), (), s32[]{:S(2)}) async-start(), calls=%async_computation.8 | async-start | bytes 8388608 | tf_op jit(solution)/shard_map/psum | solution.py:226
  1569.2 13.2 copy-start.15
  1574.2 264.7 %copy-start.1 = (bf16[1024,1024]{1,0:T(8,128)(2,1)S(1)}, bf16[1024,1024]{1,0:T(8,128)(2,1)}, u32[]{:S(2)}) copy-start(bf16[1024,1024]{1,0:T(8,128)(2,1)} %param.34) | copy-start | bytes 6291460
  (1 other events, 1.0 us)
Sparse Core Ops, SparseCore 0:
  90.0 564.0 all-gather.2
  698.4 289.0 all-reduce.4
  1032.7 289.7 all-reduce.6
  1325.7 40.0 reduce-scatter.16
  1369.0 41.1 reduce-scatter.14
  1533.3 32.8 reduce-scatter.18
  1569.3 34.2 reduce-scatter.20
  1606.6 34.1 reduce-scatter.22
  1643.9 34.1 reduce-scatter.12
  1680.3 154.9 all-reduce.8
